TPU v7x, 32 devices: a whole 2x2x4 slice. The times are simulated.
32 devices in a mesh: dp: 8 (over z, y), tp: 4 (over x, core).
Axes of the slice: x: 2, y: 2, z: 4, core: 2. Of those that a mesh axis runs over, the one named last changes fastest.
Arguments:
- tokens: bfloat16 [128, 256, 512], P('dp'), may hold values from -6 to 6
- frame_counts: int32 [128], P('dp'), may hold values from 128 to 256, as said below
- rate_groups: int32 [128], P('dp'), may hold values from 0 to 1
- conv_weight: bfloat16 [7, 512], replicated, may hold values from -2 to 2
- conv_bias: bfloat16 [512], replicated, may hold values from -3 to 3
- norm_scale: bfloat16 [2, 512], replicated, may hold values from 0.5 to 1.5
- norm_shift: bfloat16 [2, 512], replicated, may hold values from -2 to 2
- weight_in: bfloat16 [512, 1536], P(None, 'tp'), may hold values from -0.25 to 0.25
- bias_in: bfloat16 [1536], P('tp'), may hold values from -2 to 2
- weight_out: bfloat16 [1536, 512], P('tp'), may hold values from -0.21875 to 0.21875
- bias_out: bfloat16 [512], replicated, may hold values from -2 to 2
- layer_scale: bfloat16 [512], replicated, may hold values from 0.5 to 1.5
- cotangent: bfloat16 [128, 256, 512], P('dp'), may hold values from -6 to 6
Outputs:
- block_out: bfloat16 [128, 256, 512], P('dp')
- grad_tokens: float32 [128, 256, 512], P('dp')
- grad_conv_weight: float32 [7, 512], replicated
- grad_conv_bias: float32 [512], replicated
- grad_norm_scale: float32 [2, 512], replicated
- grad_norm_shift: float32 [2, 512], replicated
- grad_weight_in: float32 [512, 1536], P(None, 'tp')
- grad_bias_in: float32 [1536], P('tp')
- grad_weight_out: float32 [1536, 512], P('tp')
- grad_bias_out: float32 [512], replicated
- grad_layer_scale: float32 [512], replicated
Inputs may be any that keep to these rules, and one draw needn't show every extreme that they name: `frame_counts`: an item of group 0 has at most 256 live frames, one of group 1 at most 240; both bounds are reached, and so is the least.
All inputs are finite; a program needn't handle non-finite values.
Results may differ from a plain program's by a relative error of at most 0.0061.
Values may be sent and summed in bfloat16 or wider, within the bound.
No kernel may reach another device: no remote copies, remote signals or barrier semaphores. Data moves between devices by JAX's collectives and lax.ppermute only.
A program may use at most 192 MiB of HBM per device.

v0:
```python
import jax
import jax.numpy as jnp
from jax import lax
from jax.sharding import PartitionSpec as P

EPS = 1e-06
HIGH = lax.Precision.HIGHEST


def gelu_parts(pre_act):
    normal_cdf = 0.5 * (1.0 + lax.erf(pre_act * 0.7071067811865476))
    density = jnp.exp(-0.5 * pre_act * pre_act) * 0.3989422804014327
    return (pre_act * normal_cdf, normal_cdf + pre_act * density)


def contract_rows(left, right, precision=None):
    return lax.dot_general(
        left,
        right,
        (((0,), (0,)), ((), ())),
        precision=precision,
        preferred_element_type=jnp.float32,
    )


def contract_last(left, right):
    return lax.dot_general(
        left, right, (((1,), (1,)), ((), ())), preferred_element_type=jnp.float32
    )


def per_device(
    tokens,
    frame_counts,
    rate_groups,
    conv_weight,
    conv_bias,
    norm_scale,
    norm_shift,
    weight_in,
    bias_in,
    weight_out,
    bias_out,
    layer_scale,
    cotangent,
):
    item_count, frames, model_width = tokens.shape
    row_count = item_count * frames
    tap_count = conv_weight.shape[0]
    half_width = tap_count // 2
    rate_count = norm_scale.shape[0]
    frame_mask = (jnp.arange(frames)[None, :] < frame_counts[:, None]).astype(jnp.float32)
    masked = tokens.astype(jnp.float32) * frame_mask[..., None]
    padded = jnp.pad(masked, ((0, 0), (half_width, half_width), (0, 0)))
    conv_taps = conv_weight.astype(jnp.float32)
    conv = conv_bias.astype(jnp.float32) + conv_taps[0] * padded[:, 0:frames]
    for tap_index in range(1, tap_count):
        conv = conv + conv_taps[tap_index] * padded[:, tap_index : tap_index + frames]
    row_mean = jnp.mean(conv, axis=-1, keepdims=True)
    centered = conv - row_mean
    variance = jnp.mean(centered * centered, axis=-1, keepdims=True)
    inv_std = lax.rsqrt(variance + EPS).reshape(row_count, 1)
    normed = centered.reshape(row_count, model_width) * inv_std
    hot_items = (rate_groups[:, None] == jnp.arange(rate_count)[None, :]).astype(jnp.float32)
    hot_rows = jnp.broadcast_to(hot_items[:, None, :], (item_count, frames, rate_count)).reshape(
        row_count, rate_count
    )
    scale_table = norm_scale.astype(jnp.float32)
    shift_table = norm_shift.astype(jnp.float32)
    scale_items = jnp.dot(hot_items, scale_table, precision=HIGH)
    shift_items = jnp.dot(hot_items, shift_table, precision=HIGH)
    adapted = (
        (
            normed.reshape(item_count, frames, model_width) * scale_items[:, None, :]
            + shift_items[:, None, :]
        )
        .astype(jnp.bfloat16)
        .reshape(row_count, model_width)
    )
    pre_act = jnp.dot(adapted, weight_in, preferred_element_type=jnp.float32) + bias_in.astype(
        jnp.float32
    )
    activation, gelu_slope = gelu_parts(pre_act)
    act_low = activation.astype(jnp.bfloat16)
    masked_rows = masked.reshape(row_count, model_width)
    mask_rows = frame_mask.reshape(row_count, 1)
    grad_rows = cotangent.astype(jnp.float32).reshape(row_count, model_width) * mask_rows
    gamma = layer_scale.astype(jnp.float32)
    bias_last = bias_out.astype(jnp.float32)
    summed = lax.psum(jnp.dot(act_low, weight_out, preferred_element_type=jnp.float32), "tp")
    branch = summed + bias_last
    out_rows = ((masked_rows + gamma * branch) * mask_rows).astype(jnp.bfloat16)
    grad_gamma = jnp.sum(grad_rows * branch, axis=0)
    grad_bias_last = jnp.sum(grad_rows * gamma, axis=0)
    branch_low = (grad_rows * gamma).astype(jnp.bfloat16)
    grad_weight_out = contract_rows(act_low, branch_low)
    act_grad = contract_last(branch_low, weight_out)
    pre_grad = act_grad * gelu_slope
    grad_bias_in = jnp.sum(pre_grad, axis=0)
    pre_low = pre_grad.astype(jnp.bfloat16)
    grad_weight_in = contract_rows(adapted, pre_low)
    adapted_grad = lax.psum(contract_last(pre_low, weight_in), "tp")
    grad_scale = contract_rows(hot_rows, adapted_grad * normed, HIGH)
    grad_shift = contract_rows(hot_rows, adapted_grad, HIGH)
    normed_grad = adapted_grad * jnp.dot(hot_rows, scale_table, precision=HIGH)
    mean_grad = jnp.mean(normed_grad, axis=-1, keepdims=True)
    mean_cross = jnp.mean(normed_grad * normed, axis=-1, keepdims=True)
    conv_grad = inv_std * (normed_grad - mean_grad - normed * mean_cross)
    grad_conv_bias = jnp.sum(conv_grad, axis=0)
    tap_grads = []
    for tap_index in range(tap_count):
        shifted = padded[:, tap_index : tap_index + frames].reshape(row_count, model_width)
        tap_grads.append(jnp.sum(conv_grad * shifted, axis=0))
    grad_conv_weight = jnp.stack(tap_grads, axis=0)
    grad_padded = jnp.pad(
        conv_grad.reshape(item_count, frames, model_width),
        ((0, 0), (half_width, half_width), (0, 0)),
    )
    masked_grad = conv_taps[0] * grad_padded[:, 2 * half_width : 2 * half_width + frames]
    for tap_index in range(1, tap_count):
        offset = 2 * half_width - tap_index
        masked_grad = masked_grad + conv_taps[tap_index] * grad_padded[:, offset : offset + frames]
    grad_tokens = frame_mask[..., None] * (
        grad_rows.reshape(item_count, frames, model_width) + masked_grad
    )
    (
        grad_weight_in,
        grad_bias_in,
        grad_weight_out,
        grad_conv_weight,
        grad_conv_bias,
        grad_scale,
        grad_shift,
        grad_bias_last,
        grad_gamma,
    ) = lax.psum(
        (
            grad_weight_in,
            grad_bias_in,
            grad_weight_out,
            grad_conv_weight,
            grad_conv_bias,
            grad_scale,
            grad_shift,
            grad_bias_last,
            grad_gamma,
        ),
        "dp",
    )
    block_out = out_rows.reshape(item_count, frames, model_width)
    return (
        block_out,
        grad_tokens,
        grad_conv_weight,
        grad_conv_bias,
        grad_scale,
        grad_shift,
        grad_weight_in,
        grad_bias_in,
        grad_weight_out,
        grad_bias_last,
        grad_gamma,
    )


def solution(mesh):
    in_specs = (
        P("dp", None, None),
        P("dp"),
        P("dp"),
        P(),
        P(),
        P(),
        P(),
        P(None, "tp"),
        P("tp"),
        P("tp", None),
        P(),
        P(),
        P("dp", None, None),
    )
    out_specs = (
        P("dp", None, None),
        P("dp", None, None),
        P(),
        P(),
        P(),
        P(),
        P(None, "tp"),
        P("tp"),
        P("tp", None),
        P(),
        P(),
    )
    return jax.shard_map(
        per_device, mesh=mesh, in_specs=in_specs, out_specs=out_specs, check_vma=False
    )
```

profile of v0, /device:TPU:0, one launch (start us, length us, event | category | flops | bytes accessed | tf_op | source)
XLA Modules:
  0.0 496.8 jit_solution(17823976869492066244)
XLA Ops:
  7.2 0.0 copy-start
  7.2 0.0 all-reduce.10.cloned.1.call-start
  7.2 0.0 copy-start.6
  7.3 1.0 fusion.34
  8.3 0.0 copy-start.23
  8.3 0.0 copy-start.25
  8.3 0.0 copy-start.27
  8.3 0.0 copy-start.29
  8.3 1.0 fusion.24
  9.3 0.7 convert_element_type.68
  10.0 2.6 convert_multiply_fusion
  12.6 21.1 %fusion.33 = (f32[16,256]{1,0:T(8,128)S(1)}, f32[16,256,512]{2,1,0:T(8,128)}, f32[16,256,512]{2,1,0:T(8,128)}, f32[16,256,512]{2,1,0:T(8,128)}, f32[16,256,512]{...) fusion(f32[512]{0:T(512)S(1)} %bitcast.116, f32[512]{0:T(512)S(1)} %bitcast.114, ...), kind=kLoop, calls=%fused_computation.75 | loop fusion | flops 35647488 | bytes 71352320 | tf_op jit(solution)/shard_map/reduce_sum | solution.py:59
  33.7 0.0 copy-done.19
  33.8 0.0 copy-start.33
  33.8 0.0 copy-start.35
  33.8 0.0 copy-start.31
  33.8 0.0 copy-start.37
  33.8 0.0 copy-start.38
  33.9 4.2 multiply_reduce_fusion.3
  38.1 0.7 fusion.30
  38.7 0.0 copy-done.33
  38.7 0.2 fusion.26
  38.9 0.2 fusion.27
  39.2 0.0 copy-start.15
  39.2 1.3 add_convert_fusion
  40.5 0.0 copy-start.8
  40.5 0.0 copy-start.5
  40.5 2.9 multiply_convert_fusion.1
  43.5 0.0 copy-start.11
  43.5 1.0 copy-done.5
  44.5 1.1 multiply_convert_fusion
  45.6 5.0 %fusion.35 = (f32[384]{0:T(512)}, bf16[4096,384]{1,0:T(8,128)(2,1)S(1)}) fusion(f32[4096,384]{1,0:T(8,128)S(1)} %get-tuple-element.70, bf16[4096,512]{1,0:T(8,128)(2,1)S(1)} %multiply_convert_fusion, bf16[384,512]{1,0:T(8,128)(2,1)S(1)} %copy-done.11), kind=kOutput, calls=%fused_computation.77 | convolution fusion | flops 1627913856 | bytes 14026240 | tf_op jit(solution)/shard_map/dot_general | solution.py:27
  50.7 5.6 %fusion.21 = f32[4096,512]{1,0:T(8,128)} fusion(bf16[512,384]{1,0:T(8,128)(2,1)S(1)} %copy-done, bf16[4096,384]{1,0:T(8,128)(2,1)S(1)} %get-tuple-element.73), kind=kOutput, calls=%fused_computation.56 | convolution fusion | flops 1610612736 | bytes 11927552 | tf_op jit(solution)/shard_map/dot_general | solution.py:27
  56.3 5.7 %fusion.36 = f32[4096,512]{1,0:T(8,128)} fusion(bf16[4096,384]{1,0:T(8,128)(2,1)S(1)} %get-tuple-element.69, bf16[384,512]{1,0:T(8,128)(2,1)S(1)} %copy-done.11), kind=kOutput, calls=%fused_computation.78 | convolution fusion | flops 1610612736 | bytes 11927552 | tf_op jit(solution)/shard_map/dot_general | solution.py:90
  62.0 0.0 all-reduce.10.cloned.1.call-update
  62.1 0.2 all-reduce.8.cloned.1.call-start
  62.3 0.0 copy-start.9
  62.3 6.0 %fusion.38 = f32[384,512]{1,0:T(8,128)} fusion(bf16[4096,384]{1,0:T(8,128)(2,1)} %copy-done.10, bf16[4096,512]{1,0:T(8,128)(2,1)} %copy-done.7), kind=kOutput, calls=%fused_computation.80 | convolution fusion | flops 1610612736 | bytes 8126464 | tf_op jit(solution)/shard_map/dot_general | solution.py:17
  68.3 0.0 copy-start.32
  68.3 3.2 fusion.19
  71.5 0.0 all-reduce.8.cloned.1.call-update
  71.6 0.1 broadcast_bitcast_fusion
  71.7 282.0 %all-reduce.10.cloned.1.call-done = (f32[4096,512]{1,0:T(8,128)}, f32[4096,512]{1,0:T(8,128)}) async-done(((f32[4096,512]{1,0:T(8,128)}, f32[4096,512]{1,0:T(8,128)}), (f32[4096,512]{1,0:T(8,128)}, f32[4096,512]{1,0:T(8,128)})) %all-reduce.10.cloned.1.call-update) | async-done | bytes 16777232 | tf_op jit(solution)/shard_map/psum | solution.py:90
  353.8 7.1 %fusion.37 = f32[2,512]{1,0:T(2,128)S(1)} fusion(f32[4096,2]{0,1:T(2,128)S(1)} %bitcast.97, f32[4096,512]{1,0:T(8,128)} %get-tuple-element.31), kind=kOutput, calls=%fused_computation.79 | convolution fusion | flops 50331648 | bytes 8425472 | tf_op jit(solution)/shard_map/dot_general | solution.py:17
  360.9 0.0 copy-done.32
  360.9 0.0 copy-start.16
  360.9 11.0 %fusion.32 = (f32[4096]{0:T(1024)S(1)}, f32[4096]{0:T(1024)S(1)}, f32[4096,512]{1,0:T(8,128)}) fusion(f32[4096]{0:T(1024)S(1)} %bitcast.102, f32[16,256,512]{2,1,0:T(8,128)} %copy-done.2, f32[4096,512]{1,0:T(8,128)S(1)} %copy-done.4, f32[4096,2]{0,1:T(2,128)S(1)} %bitcast.98, bf16[2,512]{1,0:T(2,128)(2,1)S(1)} %copy-done.32), kind=kOutput, calls=%fused_computation.74 | convolution fusion | flops 60809216 | bytes 25249792 | tf_op jit(solution)/shard_map/dot_general | solution.py:105
  372.0 37.2 %multiply_reduce_fusion = (f32[512]{0:T(512)S(1)}, bf16[4096,512]{1,0:T(8,128)(2,1)}, f32[4096,512]{1,0:T(8,128)}, f32[512]{0:T(512)S(1)}, f32[512]{0:T(512)S(1)...) fusion(bf16[16,256,512]{2,1,0:T(8,128)(2,1)} %param.25, ...), kind=kLoop, calls=%fused_computation.20 | loop fusion | flops 60812800 | bytes 109139968 | tf_op jit(solution)/shard_map/reduce_sum | solution.py:93
  409.2 0.0 copy-start.24
  409.2 0.0 copy-start.26
  409.2 0.0 copy-start.28
  409.2 0.0 copy-start.30
  409.2 8.1 %fusion.9 = f32[2,512]{1,0:T(2,128)S(1)} fusion(f32[4096,2]{0,1:T(2,128)S(1)} %bitcast.99, f32[4096,512]{1,0:T(8,128)} %get-tuple-element.31, f32[4096,512]{1,0:T(8,128)} %get-tuple-element.40), kind=kOutput, calls=%fused_computation.22 | convolution fusion | flops 52428800 | bytes 16814080 | tf_op jit(solution)/shard_map/dot_general | solution.py:17
  417.4 0.0 copy-start.1
  417.4 0.0 copy-done.18
  417.4 0.0 copy-done.20
  417.4 0.0 copy-done.22
  417.5 0.0 copy-done.24
  417.5 0.0 copy-done.26
  417.5 0.0 copy-start.36
  417.5 30.6 %multiply_reduce_fusion.1 = (f32[512]{0:T(512)S(1)}, f32[16,256,512]{2,1,0:T(8,128)}) fusion(bf16[16,256,512]{2,1,0:T(8,128)(2,1)} %param.25, f32[512]{0:T(512)S(1)} %copy-done.16, f32[16,256]{1,0:T(8,128)S(1)} %get-tuple-element.68, f32[512]{0:T(512)S(1)} %bitcast.117, f32[512]{0:T(512)S(1)} %bitcast.115, f32[512]{0:T(512)S(1)} %bitcast.113, ...), kind=kLoop, calls=%fused_computation.21 | loop fusion | flops 39845376 | bytes 21006336 | tf_op jit(solution)/shard_map/reduce_sum | solution.py:94
  448.1 37.7 %all-reduce.2 = (f32[7,512]{1,0:T(8,128)}, f32[512]{0:T(512)}, f32[2,512]{1,0:T(2,128)}, f32[2,512]{1,0:T(2,128)}, f32[384]{0:T(512)}, /*index=5*/f32[512]{0:T(512)}, f32[512]{0:T(512)}) all-reduce(f32[7,512]{1,0:T(8,128)S(1)} %stack.31, f32[512]{0:T(512)S(1)} %get-tuple-element.48, ...), channel_id=1, replica_groups=mesh['dp'=8,'tp'=4] {'dp'}, use_global_device_ids=true, to_apply=%region_13.14 | all-reduce | flops 7552 | bytes 60416 | tf_op jit(solution)/shard_map/psum | solution.py:136
  485.8 2.1 copy.31
  487.9 2.1 copy.32
  (58 shorter events, 0.2 us)
Async XLA Ops:
  7.2 33.4 %copy-start = (bf16[512,384]{1,0:T(8,128)(2,1)S(1)}, bf16[512,384]{1,0:T(8,128)(2,1)}, u32[]{:S(2)}) copy-start(bf16[512,384]{1,0:T(8,128)(2,1)} %param.20) | copy-start | bytes 1179652
  7.2 346.6 %all-reduce.10.cloned.1.call-start = ((), (), s32[]{:S(2)}) async-start(), calls=%async_computation.1 | async-start | bytes 33554432 | tf_op jit(solution)/shard_map/psum | solution.py:90
  7.2 5.4 %copy-start.6 = (bf16[16,256,512]{2,1,0:T(8,128)(2,1)S(1)}, bf16[16,256,512]{2,1,0:T(8,128)(2,1)}, u32[]{:S(2)}) copy-start(bf16[16,256,512]{2,1,0:T(8,128)(2,1)} %param.13) | copy-start | bytes 12582916
  8.2 25.5 %copy-start.17 = (f32[1,512]{1,0:T(1,128)}, f32[1,512]{1,0:T(1,128)S(1)}, u32[]{:S(2)}) copy-start(f32[1,512]{1,0:T(1,128)S(1)} %get-tuple-element.60) | copy-start | bytes 6148
  8.2 25.5 %copy-start.19 = (f32[1,512]{1,0:T(1,128)}, f32[1,512]{1,0:T(1,128)S(1)}, u32[]{:S(2)}) copy-start(f32[1,512]{1,0:T(1,128)S(1)} %get-tuple-element.61) | copy-start | bytes 6148
  8.2 25.5 %copy-start.21 = (f32[1,512]{1,0:T(1,128)}, f32[1,512]{1,0:T(1,128)S(1)}, u32[]{:S(2)}) copy-start(f32[1,512]{1,0:T(1,128)S(1)} %get-tuple-element.62) | copy-start | bytes 6148
  8.3 25.5 %copy-start.23 = (f32[1,512]{1,0:T(1,128)}, f32[1,512]{1,0:T(1,128)S(1)}, u32[]{:S(2)}) copy-start(f32[1,512]{1,0:T(1,128)S(1)} %get-tuple-element.63) | copy-start | bytes 6148
  8.3 25.5 %copy-start.25 = (f32[1,512]{1,0:T(1,128)}, f32[1,512]{1,0:T(1,128)S(1)}, u32[]{:S(2)}) copy-start(f32[1,512]{1,0:T(1,128)S(1)} %get-tuple-element.64) | copy-start | bytes 6148
  8.3 25.5 %copy-start.27 = (f32[1,512]{1,0:T(1,128)}, f32[1,512]{1,0:T(1,128)S(1)}, u32[]{:S(2)}) copy-start(f32[1,512]{1,0:T(1,128)S(1)} %get-tuple-element.65) | copy-start | bytes 6148
  8.3 25.5 %copy-start.29 = (f32[1,512]{1,0:T(1,128)}, f32[1,512]{1,0:T(1,128)S(1)}, u32[]{:S(2)}) copy-start(f32[1,512]{1,0:T(1,128)S(1)} %get-tuple-element.66) | copy-start | bytes 6148
  12.6 21.2 %copy-start.3 = (f32[16,256,512]{2,1,0:T(8,128)}, f32[16,256,512]{2,1,0:T(8,128)S(1)}, u32[]{:S(2)}) copy-start(f32[16,256,512]{2,1,0:T(8,128)S(1)} %convert_multiply_fusion) | copy-start | bytes 25165828
  33.8 4.9 copy-start.33
  33.8 4.9 copy-start.35
  33.8 5.1 %copy-start.31 = (bf16[2,512]{1,0:T(2,128)(2,1)S(1)}, bf16[2,512]{1,0:T(2,128)(2,1)}, u32[]{:S(2)}) copy-start(bf16[2,512]{1,0:T(2,128)(2,1)} %param.18) | copy-start | bytes 6148
  33.8 5.3 %copy-start.37 = (bf16[384]{0:T(512)(128)(2,1)S(1)}, bf16[384]{0:T(512)(128)(2,1)}, u32[]{:S(2)}) copy-start(bf16[384]{0:T(512)(128)(2,1)} %param.21) | copy-start | bytes 2308
  33.8 5.3 %copy-start.38 = (bf16[512]{0:T(512)(128)(2,1)S(1)}, bf16[512]{0:T(512)(128)(2,1)}, u32[]{:S(2)}) copy-start(bf16[512]{0:T(512)(128)(2,1)} %param.24) | copy-start | bytes 3076
  38.1 5.4 %copy-start.2 = (f32[16,256,512]{2,1,0:T(8,128)}, f32[16,256,512]{2,1,0:T(8,128)S(1)}, u32[]{:S(2)}) copy-start(f32[16,256,512]{2,1,0:T(8,128)S(1)} %get-tuple-element.34) | copy-start | bytes 25165828
  39.2 4.4 copy-start.12
  39.2 4.3 copy-start.15
  40.5 3.0 copy-start.8
  40.5 4.0 copy-start.5
  43.5 12.8 %copy-start.10 = (bf16[4096,384]{1,0:T(8,128)(2,1)}, bf16[4096,384]{1,0:T(8,128)(2,1)S(1)}, u32[]{:S(2)}) copy-start(bf16[4096,384]{1,0:T(8,128)(2,1)S(1)} %get-tuple-element.69) | copy-start | bytes 9437188
  43.5 2.1 copy-start.11
  45.6 5.1 %copy-start.7 = (bf16[4096,512]{1,0:T(8,128)(2,1)}, bf16[4096,512]{1,0:T(8,128)(2,1)S(1)}, u32[]{:S(2)}) copy-start(bf16[4096,512]{1,0:T(8,128)(2,1)S(1)} %multiply_convert_fusion) | copy-start | bytes 12582916
  62.1 423.8 %all-reduce.8.cloned.1.call-start = ((), (), s32[]{:S(2)}) async-start(), calls=%async_computation | async-start | bytes 3145728 | tf_op jit(solution)/shard_map/psum | solution.py:136
  62.3 6.0 %copy-start.9 = (bf16[16,256,512]{2,1,0:T(8,128)(2,1)S(1)}, bf16[16,256,512]{2,1,0:T(8,128)(2,1)}, u32[]{:S(2)}) copy-start(bf16[16,256,512]{2,1,0:T(8,128)(2,1)} %copy-done.8) | copy-start | bytes 12582916
  68.3 3.3 copy-start.34
  68.3 3.3 copy-start.14
  68.3 3.4 copy-start.39
  68.3 292.6 %copy-start.32 = (bf16[2,512]{1,0:T(2,128)(2,1)S(1)}, bf16[2,512]{1,0:T(2,128)(2,1)}, u32[]{:S(2)}) copy-start(bf16[2,512]{1,0:T(2,128)(2,1)} %param.18) | copy-start | bytes 6148
  353.7 7.1 %copy-start.4 = (f32[4096,512]{1,0:T(8,128)S(1)}, f32[4096,512]{1,0:T(8,128)}, u32[]{:S(2)}) copy-start(f32[4096,512]{1,0:T(8,128)} %get-tuple-element.31) | copy-start | bytes 25165828
  360.9 11.1 %copy-start.13 = (f32[2,2,8,128]{3,1,2,0:T(2,128)S(1)}, f32[2,2,8,128]{3,1,2,0:T(2,128)}, u32[]{:S(2)}) copy-start(f32[2,2,8,128]{3,1,2,0:T(2,128)} %copy-done.12) | copy-start | bytes 49156
  360.9 11.0 %copy-start.16 = (f32[512]{0:T(512)S(1)}, f32[512]{0:T(512)}, u32[]{:S(2)}) copy-start(f32[512]{0:T(512)} %copy-done.15) | copy-start | bytes 6148
  409.2 8.3 %copy-start.18 = (f32[1,512]{1,0:T(1,128)S(1)}, f32[1,512]{1,0:T(1,128)}, u32[]{:S(2)}) copy-start(f32[1,512]{1,0:T(1,128)} %copy-done.17) | copy-start | bytes 6148
  409.2 8.3 %copy-start.20 = (f32[1,512]{1,0:T(1,128)S(1)}, f32[1,512]{1,0:T(1,128)}, u32[]{:S(2)}) copy-start(f32[1,512]{1,0:T(1,128)} %copy-done.19) | copy-start | bytes 6148
  409.2 8.3 %copy-start.22 = (f32[1,512]{1,0:T(1,128)S(1)}, f32[1,512]{1,0:T(1,128)}, u32[]{:S(2)}) copy-start(f32[1,512]{1,0:T(1,128)} %copy-done.21) | copy-start | bytes 6148
  409.2 8.3 %copy-start.24 = (f32[1,512]{1,0:T(1,128)S(1)}, f32[1,512]{1,0:T(1,128)}, u32[]{:S(2)}) copy-start(f32[1,512]{1,0:T(1,128)} %copy-done.23) | copy-start | bytes 6148
  409.2 8.3 %copy-start.26 = (f32[1,512]{1,0:T(1,128)S(1)}, f32[1,512]{1,0:T(1,128)}, u32[]{:S(2)}) copy-start(f32[1,512]{1,0:T(1,128)} %copy-done.25) | copy-start | bytes 6148
  409.2 8.3 %copy-start.28 = (f32[1,512]{1,0:T(1,128)S(1)}, f32[1,512]{1,0:T(1,128)}, u32[]{:S(2)}) copy-start(f32[1,512]{1,0:T(1,128)} %copy-done.27) | copy-start | bytes 6148
  409.2 8.3 %copy-start.30 = (f32[1,512]{1,0:T(1,128)S(1)}, f32[1,512]{1,0:T(1,128)}, u32[]{:S(2)}) copy-start(f32[1,512]{1,0:T(1,128)} %copy-done.29) | copy-start | bytes 6148
  417.4 72.5 %copy-start.1 = (bf16[512,384]{1,0:T(8,128)(2,1)S(1)}, bf16[512,384]{1,0:T(8,128)(2,1)}, u32[]{:S(2)}) copy-start(bf16[512,384]{1,0:T(8,128)(2,1)} %param.20) | copy-start | bytes 1179652
  417.5 30.6 %copy-start.36 = (f32[384]{0:T(512)S(1)}, f32[384]{0:T(512)}, u32[]{:S(2)}) copy-start(f32[384]{0:T(512)} %get-tuple-element.72) | copy-start | bytes 4612
Sparse Core Ops, SparseCore 0:
  62.2 291.5 all-reduce.9
  358.5 89.2 all-reduce.7
where the time goes:
time: 497 us
  waiting for transfers between devices  282 us (57%)
  other arithmetic  100 us (20%)
  matrix products  55.2 us (11%)
  blocking collectives  37.7 us (8%)
  between operations  14.7 us (3%)
  local copies, waits for them, and re-layouts  6.43 us (1%)
    psum x1, waiting for transfers between devices, per_device(): lax.psum(jnp.dot(act_low, weight_out, preferred_element_type=jnp.float32)...  282 us
    psum x1, blocking collectives, per_device(): lax.psum((grad_weight_in, grad_bias_in, grad_weight_out, grad_conv_weight...  37.7 us
    reduce_sum x1, other arithmetic, per_device(): grad_gamma = jnp.sum(grad_rows * branch, axis=0)  37.2 us
    reduce_sum x1, other arithmetic, per_device(): grad_bias_last = jnp.sum(grad_rows * gamma, axis=0)  30.6 us
    dot_general x4, matrix products, contract_rows(): lax.dot_general(left, right, (((0,), (0,)), ((), ())), precision=precisio...  24.5 us
    reduce_sum x1, other arithmetic, per_device(): row_mean = jnp.mean(conv, axis=-1, keepdims=True)  21.1 us
    dot_general x1, matrix products, per_device(): normed_grad = adapted_grad * jnp.dot(hot_rows, scale_table, precision=HIGH)  11 us
    dot_general x2, matrix products, contract_last(): lax.dot_general(left, right, (((1,), (1,)), ((), ())), preferred_element_...  10.6 us
  transfers between devices with their start and end apart: 2, of which 1 were waited for; matrix products, arithmetic and copies ran while one was open for 21% of the time, Pallas kernels for 0%

commit v1 on v0

--- a/solution.py
+++ b/solution.py
@@ -87,7 +87,8 @@
     grad_rows = cotangent.astype(jnp.float32).reshape(row_count, model_width) * mask_rows
     gamma = layer_scale.astype(jnp.float32)
     bias_last = bias_out.astype(jnp.float32)
-    summed = lax.psum(jnp.dot(act_low, weight_out, preferred_element_type=jnp.float32), "tp")
+    message = jnp.dot(act_low, weight_out, preferred_element_type=jnp.float32)
+    summed = jax.lax.all_gather(message, "tp").sum(axis=0)
     branch = summed + bias_last
     out_rows = ((masked_rows + gamma * branch) * mask_rows).astype(jnp.bfloat16)
     grad_gamma = jnp.sum(grad_rows * branch, axis=0)

time: 497 us -> 523 us (1.052)
  other arithmetic: 100 us -> 125 us
    psum x1, waiting for transfers between devices: 282 us -> 140 us  [per_device(): adapted_grad = lax.psum(contract_last(pre_low, weight_in), 'tp')]
    all_gather x0 -> x1, waiting for transfers between devices: none -> 139 us  [per_device(): summed = jax.lax.all_gather(message, 'tp').sum(axis=0)]
    reduce_sum x1 -> x2, other arithmetic: 30.6 us -> 55.3 us  [the longest x1 38.5 us: per_device(): grad_conv_bias = jnp.sum(conv_grad, axis=0)]
  transfers between devices with their start and end apart: 2 -> 3, of which waited for: 1 -> 3; matrix products, arithmetic and copies ran while one was open for 21% -> 26% of each run, Pallas kernels for 0% -> 0%
where the time goes in v1:
time: 523 us; the launch traced here: 522 us
  waiting for transfers between devices  281 us (54%)
  other arithmetic  125 us (24%)
  matrix products  55.1 us (11%)
  blocking collectives  38.2 us (7%)
  between operations  14.3 us (3%)
  local copies, waits for them, and re-layouts  8.75 us (2%)
    psum x1, waiting for transfers between devices, per_device(): adapted_grad = lax.psum(contract_last(pre_low, weight_in), 'tp')  140 us
    all_gather x1, waiting for transfers between devices, per_device(): summed = jax.lax.all_gather(message, 'tp').sum(axis=0)  139 us
    reduce_sum x1, other arithmetic, per_device(): grad_conv_bias = jnp.sum(conv_grad, axis=0)  38.5 us
    psum x1, blocking collectives, per_device(): lax.psum((grad_weight_in, grad_bias_in, grad_weight_out, grad_conv_weight...  38.2 us
    reduce_sum x1, other arithmetic, per_device(): grad_gamma = jnp.sum(grad_rows * branch, axis=0)  36.7 us
    dot_general x4, matrix products, contract_rows(): lax.dot_general(left, right, (((0,), (0,)), ((), ())), precision=precisio...  22.5 us
    reduce_sum x1, other arithmetic, per_device(): row_mean = jnp.mean(conv, axis=-1, keepdims=True)  21.1 us
    reduce_sum x1, other arithmetic, per_device(): summed = jax.lax.all_gather(message, 'tp').sum(axis=0)  16.8 us
  transfers between devices with their start and end apart: 3, of which 3 were waited for; matrix products, arithmetic and copies ran while one was open for 26% of the time, Pallas kernels for 0%

profile of v1, /device:TPU:0, one launch (start us, length us, event | category | flops | bytes accessed | tf_op | source)
XLA Modules:
  0.0 522.2 jit_solution(17740309782703085176)
XLA Ops:
  7.2 0.0 copy-start
  7.2 0.0 all-reduce.7.cloned.1.call-start
  7.2 0.0 copy-start.4
  7.3 1.0 fusion.34
  8.3 0.0 copy-start.21
  8.3 0.0 copy-start.23
  8.3 0.0 copy-start.25
  8.3 0.0 copy-start.27
  8.3 1.0 fusion.24
  9.3 0.7 convert_element_type.69
  10.0 2.6 convert_multiply_fusion
  12.6 21.1 %fusion.33 = (f32[16,256]{1,0:T(8,128)S(1)}, f32[16,256,512]{2,1,0:T(8,128)}, f32[16,256,512]{2,1,0:T(8,128)}, f32[16,256,512]{2,1,0:T(8,128)}, f32[16,256,512]{...) fusion(f32[512]{0:T(512)S(1)} %bitcast.113, f32[512]{0:T(512)S(1)} %bitcast.111, ...), kind=kLoop, calls=%fused_computation.73 | loop fusion | flops 35647488 | bytes 71352320 | tf_op jit(solution)/shard_map/reduce_sum | solution.py:59
  33.7 0.0 copy-done.15
  33.8 0.0 copy-start.33
  33.8 0.0 copy-start.35
  33.8 0.0 copy-start.31
  33.8 0.0 copy-start.37
  33.8 0.0 copy-start.38
  33.9 4.2 multiply_reduce_fusion.3
  38.1 0.7 fusion.30
  38.7 0.2 fusion.26
  38.9 0.2 fusion.27
  39.2 0.0 copy-start.29
  39.2 1.3 add_convert_fusion
  40.5 0.0 copy-start.8
  40.5 0.0 copy-start.6
  40.5 2.9 multiply_convert_fusion.1
  43.5 0.0 copy-start.12
  43.5 0.9 copy-done.6
  44.5 1.1 fusion.8
  45.6 5.1 fusion.35
  50.6 1.6 copy-done.10
  52.3 5.6 %fusion.21 = f32[4096,512]{1,0:T(8,128)} fusion(bf16[512,384]{1,0:T(8,128)(2,1)S(1)} %copy-done, bf16[4096,384]{1,0:T(8,128)(2,1)S(1)} %get-tuple-element.61), kind=kOutput, calls=%fused_computation.54 | convolution fusion | flops 1610612736 | bytes 11927552 | tf_op jit(solution)/shard_map/dot_general | solution.py:27
  57.8 0.0 all-reduce.7.cloned.1.call-update
  57.9 0.2 all-gather.3.cloned.1.call-start
  58.1 0.7 copy-done.13
  58.8 5.7 %fusion.36 = f32[4096,512]{1,0:T(8,128)} fusion(bf16[4096,384]{1,0:T(8,128)(2,1)S(1)} %get-tuple-element.57, bf16[384,512]{1,0:T(8,128)(2,1)S(1)} %copy-done.13), kind=kOutput, calls=%fused_computation.76 | convolution fusion | flops 1610612736 | bytes 11927552 | tf_op jit(solution)/shard_map/dot_general | solution.py:90
  64.6 0.0 all-gather.3.cloned.1.call-update
  64.6 0.0 all-reduce.9.cloned.1.call-start
  64.6 0.0 copy-start.9
  64.7 5.8 %fusion.38 = f32[384,512]{1,0:T(8,128)} fusion(bf16[4096,384]{1,0:T(8,128)(2,1)S(1)} %get-tuple-element.57, bf16[4096,512]{1,0:T(8,128)(2,1)} %copy-done.7), kind=kOutput, calls=%fused_computation.78 | convolution fusion | flops 1610612736 | bytes 8126464 | tf_op jit(solution)/shard_map/dot_general | solution.py:17
  70.5 0.0 copy-start.39
  70.5 0.0 copy-start.32
  70.5 3.2 fusion.19
  73.7 0.0 all-reduce.9.cloned.1.call-update
  73.8 0.1 broadcast_bitcast_fusion
  73.9 139.6 %all-reduce.7.cloned.1.call-done = f32[4096,512]{1,0:T(8,128)} async-done(((f32[4096,512]{1,0:T(8,128)}), f32[4096,512]{1,0:T(8,128)}) %all-reduce.7.cloned.1.call-update) | async-done | bytes 8388624 | tf_op jit(solution)/shard_map/psum | solution.py:103
  213.6 12.9 %fusion.32 = (f32[4096]{0:T(1024)S(1)}, f32[4096]{0:T(1024)S(1)}, f32[4096,512]{1,0:T(8,128)}) fusion(f32[4096]{0:T(1024)S(1)} %bitcast.98, f32[16,256,512]{2,1,0:T(8,128)} %copy-done.2, f32[4096,512]{1,0:T(8,128)} %all-reduce.7.cloned.1.call-done, f32[4096,2]{0,1:T(2,128)S(1)} %bitcast.95, bf16[2,512]{1,0:T(2,128)(2,1)S(1)} %copy-done.32), kind=kOutput, calls=%fused_computation.72 | convolution fusion | flops 60809216 | bytes 25249792 | tf_op jit(solution)/shard_map/dot_general | solution.py:106
  226.5 38.5 %fusion.31 = (f32[512]{0:T(512)S(1)}, f32[512]{0:T(512)S(1)}, f32[512]{0:T(512)S(1)}, f32[512]{0:T(512)S(1)}, f32[512]{0:T(512)S(1)}, /*index=5*/f32[512]{0:T(51...) fusion(f32[16,256,512]{2,1,0:T(8,128)} %get-tuple-element.43, ...), kind=kLoop, calls=%fused_computation.71 | loop fusion | flops 41938944 | bytes 92340224 | tf_op jit(solution)/shard_map/reduce_sum | solution.py:110
  265.0 6.5 %fusion.37 = f32[2,512]{1,0:T(2,128)S(1)} fusion(f32[4096,2]{0,1:T(2,128)S(1)} %bitcast.96, f32[4096,512]{1,0:T(8,128)} %all-reduce.7.cloned.1.call-done), kind=kOutput, calls=%fused_computation.77 | convolution fusion | flops 50331648 | bytes 8425472 | tf_op jit(solution)/shard_map/dot_general | solution.py:17
  271.6 0.0 copy-done.5
  271.6 6.9 %fusion.9 = f32[2,512]{1,0:T(2,128)S(1)} fusion(f32[4096,2]{0,1:T(2,128)S(1)} %bitcast.97, f32[4096,512]{1,0:T(8,128)} %all-reduce.7.cloned.1.call-done, f32[4096,512]{1,0:T(8,128)S(1)} %copy-done.5), kind=kOutput, calls=%fused_computation.21 | convolution fusion | flops 52428800 | bytes 16814080 | tf_op jit(solution)/shard_map/dot_general | solution.py:17
  278.5 138.9 %all-gather.3.cloned.1.call-done = f32[16384,512]{1,0:T(8,128)} async-done(((f32[4096,512]{1,0:T(8,128)}), f32[16384,512]{1,0:T(8,128)}) %all-gather.3.cloned.1.call-update) | async-done | bytes 33554448 | tf_op jit(solution)/shard_map/all_gather | solution.py:91
  417.4 0.0 copy-start.26
  417.4 0.0 copy-start.28
  417.5 0.0 copy-start.30
  417.5 16.8 %reduce_sum.148 = f32[4096,512]{1,0:T(8,128)} reduce(f32[4,4096,512]{2,1,0:T(8,128)} %bitcast.91, f32[]{:T(128)} %constant.8.clone.1), dimensions={0}, to_apply=%region_2.3 | reduce | flops 6291456 | bytes 41943044 | tf_op jit(solution)/shard_map/reduce_sum | solution.py:91
  434.4 0.0 copy-start.36
  434.4 0.0 copy-start.1
  434.4 36.7 %multiply_reduce_fusion = (f32[512]{0:T(512)S(1)}, f32[512]{0:T(512)S(1)}, f32[16,256,512]{2,1,0:T(8,128)}, bf16[16,256,512]{2,1,0:T(8,128)(2,1)}) fusion(f32[4096,512]{1,0:T(8,128)} %reduce_sum.148, bf16[16,256,512]{2,1,0:T(8,128)(2,1)} %param.25, f32[512]{0:T(512)S(1)} %convert_element_type.74, f32[16,256]{1,0:T(8,128)S(1)} %get-tuple-element.56, ...), kind=kLoop, calls=%fused_computation.19 | loop fusion | flops 58719232 | bytes 37787648 | tf_op jit(solution)/shard_map/reduce_sum | solution.py:94
  471.1 38.2 %all-reduce.2 = (f32[7,512]{1,0:T(8,128)}, f32[512]{0:T(512)}, f32[2,512]{1,0:T(2,128)}, f32[2,512]{1,0:T(2,128)}, f32[384]{0:T(512)}, /*index=5*/f32[512]{0:T(512)}, f32[512]{0:T(512)}) all-reduce(f32[7,512]{1,0:T(8,128)S(1)} %stack.31, f32[512]{0:T(512)S(1)} %get-tuple-element.11, ...), channel_id=1, replica_groups=mesh['dp'=8,'tp'=4] {'dp'}, use_global_device_ids=true, to_apply=%region_13.14 | all-reduce | flops 7552 | bytes 60416 | tf_op jit(solution)/shard_map/psum | solution.py:137
  509.3 2.2 all-reduce.9.cloned.1.call-done
  511.5 2.1 copy.30
  513.6 2.1 copy.31
  (62 shorter events, 0.2 us)
Async XLA Ops:
  7.2 33.3 %copy-start = (bf16[512,384]{1,0:T(8,128)(2,1)S(1)}, bf16[512,384]{1,0:T(8,128)(2,1)}, u32[]{:S(2)}) copy-start(bf16[512,384]{1,0:T(8,128)(2,1)} %param.20) | copy-start | bytes 1179652
  7.2 206.4 %all-reduce.7.cloned.1.call-start = ((), (), s32[]{:S(2)}) async-start(), calls=%async_computation | async-start | bytes 16777216 | tf_op jit(solution)/shard_map/psum | solution.py:103
  7.2 5.4 %copy-start.4 = (bf16[16,256,512]{2,1,0:T(8,128)(2,1)S(1)}, bf16[16,256,512]{2,1,0:T(8,128)(2,1)}, u32[]{:S(2)}) copy-start(bf16[16,256,512]{2,1,0:T(8,128)(2,1)} %param.13) | copy-start | bytes 12582916
  8.2 25.5 %copy-start.15 = (f32[1,512]{1,0:T(1,128)}, f32[1,512]{1,0:T(1,128)S(1)}, u32[]{:S(2)}) copy-start(f32[1,512]{1,0:T(1,128)S(1)} %get-tuple-element.48) | copy-start | bytes 6148
  8.2 25.5 %copy-start.17 = (f32[1,512]{1,0:T(1,128)}, f32[1,512]{1,0:T(1,128)S(1)}, u32[]{:S(2)}) copy-start(f32[1,512]{1,0:T(1,128)S(1)} %get-tuple-element.49) | copy-start | bytes 6148
  8.2 25.5 %copy-start.19 = (f32[1,512]{1,0:T(1,128)}, f32[1,512]{1,0:T(1,128)S(1)}, u32[]{:S(2)}) copy-start(f32[1,512]{1,0:T(1,128)S(1)} %get-tuple-element.50) | copy-start | bytes 6148
  8.3 25.5 %copy-start.21 = (f32[1,512]{1,0:T(1,128)}, f32[1,512]{1,0:T(1,128)S(1)}, u32[]{:S(2)}) copy-start(f32[1,512]{1,0:T(1,128)S(1)} %get-tuple-element.51) | copy-start | bytes 6148
  8.3 25.5 %copy-start.23 = (f32[1,512]{1,0:T(1,128)}, f32[1,512]{1,0:T(1,128)S(1)}, u32[]{:S(2)}) copy-start(f32[1,512]{1,0:T(1,128)S(1)} %get-tuple-element.52) | copy-start | bytes 6148
  8.3 25.5 %copy-start.25 = (f32[1,512]{1,0:T(1,128)}, f32[1,512]{1,0:T(1,128)S(1)}, u32[]{:S(2)}) copy-start(f32[1,512]{1,0:T(1,128)S(1)} %get-tuple-element.53) | copy-start | bytes 6148
  8.3 25.5 %copy-start.27 = (f32[1,512]{1,0:T(1,128)}, f32[1,512]{1,0:T(1,128)S(1)}, u32[]{:S(2)}) copy-start(f32[1,512]{1,0:T(1,128)S(1)} %get-tuple-element.54) | copy-start | bytes 6148
  12.6 21.1 %copy-start.3 = (f32[16,256,512]{2,1,0:T(8,128)}, f32[16,256,512]{2,1,0:T(8,128)S(1)}, u32[]{:S(2)}) copy-start(f32[16,256,512]{2,1,0:T(8,128)S(1)} %convert_multiply_fusion) | copy-start | bytes 25165828
  33.8 5.0 copy-start.33
  33.8 4.9 copy-start.35
  33.8 5.1 copy-start.31
  33.8 5.3 %copy-start.37 = (bf16[384]{0:T(512)(128)(2,1)S(1)}, bf16[384]{0:T(512)(128)(2,1)}, u32[]{:S(2)}) copy-start(bf16[384]{0:T(512)(128)(2,1)} %param.21) | copy-start | bytes 2308
  33.8 5.3 %copy-start.38 = (bf16[512]{0:T(512)(128)(2,1)S(1)}, bf16[512]{0:T(512)(128)(2,1)}, u32[]{:S(2)}) copy-start(bf16[512]{0:T(512)(128)(2,1)} %param.24) | copy-start | bytes 3076
  38.1 5.4 %copy-start.2 = (f32[16,256,512]{2,1,0:T(8,128)}, f32[16,256,512]{2,1,0:T(8,128)S(1)}, u32[]{:S(2)}) copy-start(f32[16,256,512]{2,1,0:T(8,128)S(1)} %get-tuple-element.34) | copy-start | bytes 25165828
  39.2 4.3 copy-start.29
  40.5 3.0 copy-start.8
  40.5 3.9 copy-start.6
  43.5 2.1 copy-start.12
  45.6 5.1 copy-start.7
  50.6 1.6 copy-start.10
  57.8 1.0 copy-start.13
  57.9 359.6 %all-gather.3.cloned.1.call-start = ((), (), s32[]{:S(2)}) async-start(), calls=%async_computation.1 | async-start | bytes 41943040 | tf_op jit(solution)/shard_map/all_gather | solution.py:91
  64.6 446.9 %all-reduce.9.cloned.1.call-start = ((), (), s32[]{:S(2)}) async-start(), calls=%async_computation.2 | async-start | bytes 3145728 | tf_op jit(solution)/shard_map/psum | solution.py:137
  64.6 5.8 %copy-start.9 = (bf16[16,256,512]{2,1,0:T(8,128)(2,1)S(1)}, bf16[16,256,512]{2,1,0:T(8,128)(2,1)}, u32[]{:S(2)}) copy-start(bf16[16,256,512]{2,1,0:T(8,128)(2,1)} %copy-done.8) | copy-start | bytes 12582916
  64.7 5.8 %copy-start.11 = (bf16[4096,384]{1,0:T(8,128)(2,1)S(1)}, bf16[4096,384]{1,0:T(8,128)(2,1)}, u32[]{:S(2)}) copy-start(bf16[4096,384]{1,0:T(8,128)(2,1)} %copy-done.10) | copy-start | bytes 9437188
  70.5 3.3 copy-start.34
  70.5 3.3 copy-start.14
  70.5 3.4 copy-start.39
  70.5 143.1 %copy-start.32 = (bf16[2,512]{1,0:T(2,128)(2,1)S(1)}, bf16[2,512]{1,0:T(2,128)(2,1)}, u32[]{:S(2)}) copy-start(bf16[2,512]{1,0:T(2,128)(2,1)} %param.18) | copy-start | bytes 6148
  265.0 6.5 %copy-start.5 = (f32[4096,512]{1,0:T(8,128)S(1)}, f32[4096,512]{1,0:T(8,128)}, u32[]{:S(2)}) copy-start(f32[4096,512]{1,0:T(8,128)} %get-tuple-element.37) | copy-start | bytes 25165828
  417.4 16.9 %copy-start.16 = (f32[1,512]{1,0:T(1,128)S(1)}, f32[1,512]{1,0:T(1,128)}, u32[]{:S(2)}) copy-start(f32[1,512]{1,0:T(1,128)} %copy-done.15) | copy-start | bytes 6148
  417.4 16.9 %copy-start.18 = (f32[1,512]{1,0:T(1,128)S(1)}, f32[1,512]{1,0:T(1,128)}, u32[]{:S(2)}) copy-start(f32[1,512]{1,0:T(1,128)} %copy-done.17) | copy-start | bytes 6148
  417.4 16.9 %copy-start.20 = (f32[1,512]{1,0:T(1,128)S(1)}, f32[1,512]{1,0:T(1,128)}, u32[]{:S(2)}) copy-start(f32[1,512]{1,0:T(1,128)} %copy-done.19) | copy-start | bytes 6148
  417.4 16.9 %copy-start.22 = (f32[1,512]{1,0:T(1,128)S(1)}, f32[1,512]{1,0:T(1,128)}, u32[]{:S(2)}) copy-start(f32[1,512]{1,0:T(1,128)} %copy-done.21) | copy-start | bytes 6148
  417.4 16.9 %copy-start.24 = (f32[1,512]{1,0:T(1,128)S(1)}, f32[1,512]{1,0:T(1,128)}, u32[]{:S(2)}) copy-start(f32[1,512]{1,0:T(1,128)} %copy-done.23) | copy-start | bytes 6148
  417.4 16.9 %copy-start.26 = (f32[1,512]{1,0:T(1,128)S(1)}, f32[1,512]{1,0:T(1,128)}, u32[]{:S(2)}) copy-start(f32[1,512]{1,0:T(1,128)} %copy-done.25) | copy-start | bytes 6148
  417.4 16.9 %copy-start.28 = (f32[1,512]{1,0:T(1,128)S(1)}, f32[1,512]{1,0:T(1,128)}, u32[]{:S(2)}) copy-start(f32[1,512]{1,0:T(1,128)} %copy-done.27) | copy-start | bytes 6148
  417.5 16.9 %copy-start.30 = (f32[512]{0:T(512)S(1)}, f32[512]{0:T(512)}, u32[]{:S(2)}) copy-start(f32[512]{0:T(512)} %copy-done.29) | copy-start | bytes 6148
  434.4 36.7 %copy-start.36 = (f32[384]{0:T(512)S(1)}, f32[384]{0:T(512)}, u32[]{:S(2)}) copy-start(f32[384]{0:T(512)} %get-tuple-element.60) | copy-start | bytes 4612
  434.4 81.3 %copy-start.1 = (bf16[512,384]{1,0:T(8,128)(2,1)S(1)}, bf16[512,384]{1,0:T(8,128)(2,1)}, u32[]{:S(2)}) copy-start(bf16[512,384]{1,0:T(8,128)(2,1)} %param.20) | copy-start | bytes 1179652
Sparse Core Ops, SparseCore 0:
  58.0 155.5 all-reduce.6
  215.7 201.6 all-gather.2
  422.1 89.3 all-reduce.8
